TPU v7x, 32 devices: a whole 2x2x4 slice. The times are simulated.
32 devices in a mesh: wide: 8 (over z, y), mp: 4 (over x, core).
Axes of the slice: x: 2, y: 2, z: 4, core: 2. Of those that a mesh axis runs over, the one named last changes fastest.
Arguments:
- clip_feats: bfloat16 [1024, 768], P('wide'), may hold values from -6 to 6
- teacher_audio: bfloat16 [1024, 512], P('wide'), may hold values from -16 to 16
- teacher_text: bfloat16 [1024, 512], P(('wide', 'mp')), may hold values from -16 to 16
- w_first: bfloat16 [768, 512], P(None, 'mp'), may hold values from -0.21875 to 0.21875
- w_second: bfloat16 [512, 512], P('mp'), may hold values from -0.25 to 0.25
- pairing: int32 [1024], P('wide'), may hold values from 0 to 1023
Outputs:
- loss: float32 [], replicated
- grad_first: float32 [768, 512], P(None, 'mp')
- grad_second: float32 [512, 512], P('mp')
All inputs are finite; a program needn't handle non-finite values.
Results may differ from a plain program's by a relative error of at most 0.0052.
Values may be sent and summed in bfloat16 or wider, within the bound.
No kernel may reach another device: no remote copies, remote signals or barrier semaphores. Data moves between devices by JAX's collectives and lax.ppermute only.
A program may use at most 64 MiB of HBM per device.

v0:
```python
import math
import jax
import jax.numpy as jnp
from jax import lax
from jax.sharding import PartitionSpec as P

teacher_scale = 14.0
student_scale = 64.0
eps = 1e-06


def normalize(values):
    return values / jnp.sqrt(jnp.sum(values * values, axis=1, keepdims=True) + eps)


def inner_rows(left, right):
    return lax.dot_general(
        left, right, (((1,), (1,)), ((), ())), preferred_element_type=jnp.float32
    )


def sweep(work, initial, source, base):
    count = source.shape[0]
    width = math.gcd(count, 2048)
    block_count = count // width

    def advance(index, carry):
        block = lax.dynamic_slice_in_dim(source, index * width, width, 0)
        return work(carry, block, base + index * width)

    return lax.fori_loop(0, block_count, advance, initial)


def body(clip_feats, teacher_audio, teacher_text, w_first, w_second, pairing):
    row_count = clip_feats.shape[0]
    total = row_count * lax.axis_size("wide")
    quarter = teacher_text.shape[0]
    mp_size = lax.axis_size("mp")
    mp_index = lax.axis_index("mp")
    pre_act = jnp.dot(clip_feats, w_first, preferred_element_type=jnp.float32)
    gelu_out, gelu_back = jax.vjp(lambda u: jax.nn.gelu(u, approximate=False), pre_act)
    hidden = gelu_out.astype(jnp.bfloat16)
    raw = lax.psum(jnp.dot(hidden, w_second, preferred_element_type=jnp.float32), "mp")
    norm = jnp.sqrt(jnp.sum(raw * raw, axis=1, keepdims=True) + eps)
    student = raw / norm
    stacked = jnp.concatenate(
        [
            normalize(teacher_audio.astype(jnp.float32)).astype(jnp.bfloat16),
            student.astype(jnp.bfloat16),
        ],
        axis=0,
    )
    capt_local = normalize(teacher_text.astype(jnp.float32)).astype(jnp.bfloat16)

    def logits(block, start):
        scores = inner_rows(stacked, block)
        local_ids = start + jnp.arange(block.shape[0], dtype=jnp.int32)
        global_ids = (
            local_ids // quarter * (quarter * mp_size) + mp_index * quarter + local_ids % quarter
        )
        hit = global_ids[None, :] == pairing[:, None]
        return (teacher_scale * scores[:row_count], student_scale * scores[row_count:], hit)

    def first_pass(carry, block, start):
        tlog, slog, hit = logits(block, start)
        texp = jnp.exp(tlog)
        sexp = jnp.exp(slog)
        return (
            carry[0] + jnp.sum(texp, axis=1),
            carry[1] + jnp.sum(sexp, axis=1),
            carry[2] + jnp.sum(texp * (tlog - slog), axis=1),
            carry[3] + jnp.sum(jnp.where(hit, slog, 0.0), axis=1),
        )

    zeros_row = jnp.zeros((row_count,), jnp.float32)
    first_init = (zeros_row, zeros_row, zeros_row, zeros_row)
    zeros_grad = jnp.zeros((row_count, stacked.shape[1]), jnp.float32)

    def make_second(zt_sum, zs_sum):

        def second_pass(carry, block, start):
            tlog, slog, hit = logits(block, start)
            coef = (
                2.0 * jnp.exp(slog) / zs_sum[:, None]
                - jnp.exp(tlog) / zt_sum[:, None]
                - hit.astype(jnp.float32)
            ).astype(jnp.bfloat16)
            return carry + jnp.dot(coef, block, preferred_element_type=jnp.float32)

        return second_pass

    gathered = lax.all_gather(capt_local, "wide", axis=0, tiled=True)
    partial_stats = sweep(first_pass, first_init, gathered, 0)
    zt_sum, zs_sum, acc_sum, spair = lax.psum(partial_stats, "mp")
    second_pass = make_second(zt_sum, zs_sum)
    dpart = sweep(second_pass, zeros_grad, gathered, 0)
    loss_part = jnp.sum(acc_sum / zt_sum - jnp.log(zt_sum) + 2.0 * jnp.log(zs_sum) - spair)
    dstud = lax.psum(dpart, "mp") * (student_scale / total)
    draw = ((dstud - student * jnp.sum(student * dstud, axis=1, keepdims=True)) / norm).astype(
        jnp.bfloat16
    )
    grad_second = jnp.dot(hidden.T, draw, preferred_element_type=jnp.float32)
    dhid = lax.dot_general(
        draw, w_second, (((1,), (1,)), ((), ())), preferred_element_type=jnp.float32
    )
    dpre = gelu_back(dhid)[0].astype(jnp.bfloat16)
    grad_first = jnp.dot(clip_feats.T, dpre, preferred_element_type=jnp.float32)
    grad_first, grad_second, loss_sum = lax.psum((grad_first, grad_second, loss_part), "wide")
    return (loss_sum / total, grad_first, grad_second)


def solution(mesh):
    return jax.shard_map(
        body,
        mesh=mesh,
        in_specs=(
            P("wide", None),
            P("wide", None),
            P(("wide", "mp"), None),
            P(None, "mp"),
            P("mp", None),
            P("wide"),
        ),
        out_specs=(P(), P(None, "mp"), P("mp", None)),
        check_vma=False,
    )
```

profile of v0, /device:TPU:0, one launch (start us, length us, event | category | flops | bytes accessed | tf_op | source)
XLA Modules:
  0.0 175.5 jit_solution(1740384706962114284)
XLA Ops:
  7.2 0.0 copy-start
  7.2 0.0 copy-start.5
  7.2 0.0 all-reduce.6.cloned.1.call-start
  7.2 0.9 copy-done
  8.1 1.3 multiply_convert_fusion
  9.4 0.0 copy-done.5
  9.4 0.9 fusion.47
  10.2 0.0 copy-start.3
  10.2 0.0 all-reduce.6.cloned.1.call-update
  10.3 0.0 all-reduce.8.cloned.1.call-start
  10.3 0.8 copy-done.3
  11.1 0.0 copy-start.6
  11.1 0.1 fusion
  11.3 0.6 copy-done.6
  11.9 0.1 fusion.13
  12.0 0.1 fusion.14
  12.1 0.1 fusion.1
  12.2 32.6 %all_gather.3 = bf16[256,512]{1,0:T(8,128)(2,1)S(1)} all-gather(bf16[32,512]{1,0:T(8,128)(2,1)S(1)} %fusion.14), channel_id=1, replica_groups=mesh['wide'=8,'mp'=4] {'wide'}, dimensions={0}, use_global_device_ids=true | all-gather | bytes 294912 | tf_op jit(solution)/shard_map/all_gather | solution.py:92
  44.8 1.1 all-reduce.6.cloned.1.call-done
  45.9 0.0 copy-start.1
  45.9 1.1 multiply_reduce_fusion.1
  47.1 0.0 copy-done.1
  47.1 0.1 fusion.43
  47.2 0.0 copy-start.7
  47.2 0.3 fusion.2
  47.5 0.4 copy-done.7
  47.8 0.1 multiply_reduce_fusion.2
  48.0 5.8 %all-reduce.1 = (f32[128]{0:T(128)S(1)}, f32[128]{0:T(128)S(1)}, f32[128]{0:T(128)S(1)}, f32[128]{0:T(128)S(1)}) all-reduce(f32[128]{0:T(128)S(1)} %get-tuple-element.46, f32[128]{0:T(128)S(1)} %get-tuple-element.47, f32[128]{0:T(128)S(1)} %get-tuple-element.48, f32[128]{0:T(128)S(1)} %get-tuple-element.45), channel_id=1, replica_groups=mesh['wide'=8,'mp'=4] {'mp'}, use_global_device_ids=true, to_apply=%region_11.12 | all-reduce | flops 512 | bytes 4096 | tf_op jit(solution)/shard_map/psum | solution.py:94
  53.7 1.0 fusion.11
  54.7 0.0 all-reduce.8.cloned.1.call-update
  54.7 0.0 all-reduce.10.cloned.1.call-start
  54.8 32.4 %all-reduce.8.cloned.1.call-done = f32[128,512]{1,0:T(8,128)} async-done(((f32[128,512]{1,0:T(8,128)}), f32[128,512]{1,0:T(8,128)}) %all-reduce.8.cloned.1.call-update) | async-done | bytes 262160 | tf_op jit(solution)/shard_map/psum | solution.py:98
  87.2 0.0 copy-start.2
  87.2 1.2 multiply_reduce_fusion
  88.4 0.0 copy-done.2
  88.4 0.1 divide_convert_fusion
  88.6 0.9 fusion.48
  89.5 1.3 convolution_bitcast_fusion
  90.7 0.0 all-reduce.10.cloned.1.call-update
  90.8 0.6 subtract_reduce_fusion
  91.4 22.2 %psum.68 = f32[]{:T(128)} all-reduce(f32[]{:T(128)} %subtract_reduce_fusion), channel_id=1, replica_groups=mesh['wide'=8,'mp'=4] {'wide'}, use_global_device_ids=true, to_apply=%region_13.14 | all-reduce | flops 1 | bytes 8 | tf_op jit(solution)/shard_map/psum | solution.py:108
  114.3 50.9 %all-reduce.10.cloned.1.call-done = (f32[768,128]{0,1:T(8,128)}, f32[128,512]{1,0:T(8,128)}) async-done(((f32[768,128]{0,1:T(8,128)}, f32[128,512]{1,0:T(8,128)}), (f32[768,128]{0,1:T(8,128)}, f32[128,512]{1,0:T(8,128)})) %all-reduce.10.cloned.1.call-update) | async-done | bytes 655376 | tf_op jit(solution)/shard_map/psum | solution.py:108
  165.2 0.0 copy-start.4
  165.2 2.0 %copy.9 = f32[768,128]{1,0:T(8,128)} copy(f32[768,128]{0,1:T(8,128)} %get-tuple-element.58) | data formatting | bytes 786432
  167.1 0.0 copy-done.4
  167.1 0.7 copy.14
  (4 shorter events, 0.0 us)
Async XLA Ops:
  7.2 0.9 copy-start
  7.2 2.2 %copy-start.5 = (bf16[128,512]{1,0:T(8,128)(2,1)S(1)}, bf16[128,512]{1,0:T(8,128)(2,1)}, u32[]{:S(2)}) copy-start(bf16[128,512]{1,0:T(8,128)(2,1)} %param.10) | copy-start | bytes 393220
  7.2 38.7 %all-reduce.6.cloned.1.call-start = ((), (), s32[]{:S(2)}) async-start(), calls=%async_computation | async-start | bytes 524288 | tf_op jit(solution)/shard_map/psum | solution.py:43
  10.2 0.9 copy-start.3
  10.3 76.9 %all-reduce.8.cloned.1.call-start = ((), (), s32[]{:S(2)}) async-start(), calls=%async_computation.1 | async-start | bytes 524288 | tf_op jit(solution)/shard_map/psum | solution.py:98
  11.1 0.8 copy-start.6
  45.9 1.1 copy-start.1
  47.2 0.7 copy-start.7
  54.7 110.4 %all-reduce.10.cloned.1.call-start = ((), (), s32[]{:S(2)}) async-start(), calls=%async_computation.2 | async-start | bytes 1310720 | tf_op jit(solution)/shard_map/psum | solution.py:108
  87.2 1.2 copy-start.2
  165.2 2.0 %copy-start.4 = (f32[128,512]{1,0:T(8,128)S(1)}, f32[128,512]{1,0:T(8,128)}, u32[]{:S(2)}) copy-start(f32[128,512]{1,0:T(8,128)} %get-tuple-element.77) | copy-start | bytes 786436
Sparse Core Ops, SparseCore 0:
  10.9 34.9 all-reduce.5
  54.9 32.3 all-reduce.7
  91.3 73.8 all-reduce.9
where the time goes:
time: 176 us; the launch traced here: 175 us
  waiting for transfers between devices  84.5 us (48%)
  blocking collectives  60.5 us (34%)
  between operations  15.7 us (9%)
  matrix products  5.56 us (3%)
  local copies, waits for them, and re-layouts  5.38 us (3%)
  other arithmetic  3.71 us (2%)
    psum x1, waiting for transfers between devices, body(): lax.psum((grad_first, grad_second, loss_part), 'wide')  50.9 us
    all_gather x1, blocking collectives, body(): gathered = lax.all_gather(capt_local, 'wide', axis=0, tiled=True)  32.6 us
    psum x1, waiting for transfers between devices, body(): dstud = lax.psum(dpart, 'mp') * (student_scale / total)  32.4 us
    psum x1, blocking collectives, body(): lax.psum((grad_first, grad_second, loss_part), 'wide')  22.2 us
    psum x1, blocking collectives, body(): zt_sum, zs_sum, acc_sum, spair = lax.psum(partial_stats, 'mp')  5.76 us
    unnamed x18, local copies, waits for them, and re-layouts  5.38 us
  transfers between devices with their start and end apart: 3, of which 3 were waited for; matrix products, arithmetic and copies ran while one was open for 1% of the time, Pallas kernels for 0%

commit v1 on v0

--- a/solution.py
+++ b/solution.py
@@ -95,7 +95,7 @@
     second_pass = make_second(zt_sum, zs_sum)
     dpart = sweep(second_pass, zeros_grad, gathered, 0)
     loss_part = jnp.sum(acc_sum / zt_sum - jnp.log(zt_sum) + 2.0 * jnp.log(zs_sum) - spair)
-    dstud = lax.psum(dpart, "mp") * (student_scale / total)
+    dstud = jnp.sum(lax.all_gather(dpart, "mp"), axis=0) * (student_scale / total)
     draw = ((dstud - student * jnp.sum(student * dstud, axis=1, keepdims=True)) / norm).astype(
         jnp.bfloat16
     )

time: 176 us -> 160 us (0.909)
  waiting for transfers between devices: 84.5 us -> 68.6 us
    psum x1 -> x0, waiting for transfers between devices: 32.4 us -> none  [body(): dstud = lax.psum(dpart, 'mp') * (student_scale / total)]
    all_gather x0 -> x1, waiting for transfers between devices: none -> 16.8 us  [body(): lax.all_gather(dpart, 'mp')]
    unnamed x18 -> x16, local copies, waits for them, and re-layouts: 5.38 us -> 5.38 us
where the time goes in v1:
time: 160 us
  waiting for transfers between devices  68.6 us (43%)
  blocking collectives  60.5 us (38%)
  between operations  15.7 us (10%)
  matrix products  5.56 us (3%)
  local copies, waits for them, and re-layouts  5.38 us (3%)
  other arithmetic  4.02 us (3%)
    psum x1, waiting for transfers between devices, body(): lax.psum((grad_first, grad_second, loss_part), 'wide')  50.5 us
    all_gather x1, blocking collectives, body(): gathered = lax.all_gather(capt_local, 'wide', axis=0, tiled=True)  32.6 us
    psum x1, blocking collectives, body(): lax.psum((grad_first, grad_second, loss_part), 'wide')  22.2 us
    all_gather x1, waiting for transfers between devices, body(): lax.all_gather(dpart, 'mp')  16.8 us
    psum x1, blocking collectives, body(): zt_sum, zs_sum, acc_sum, spair = lax.psum(partial_stats, 'mp')  5.76 us
    unnamed x16, local copies, waits for them, and re-layouts  5.38 us
  transfers between devices with their start and end apart: 3, of which 3 were waited for; matrix products, arithmetic and copies ran while one was open for 1% of the time, Pallas kernels for 0%

profile of v1, /device:TPU:0, one launch (start us, length us, event | category | flops | bytes accessed | tf_op | source)
XLA Modules:
  0.0 159.8 jit_solution(12057231874256509596)
XLA Ops:
  7.2 0.0 copy-start
  7.2 0.0 copy-start.4
  7.2 0.0 all-reduce.5.cloned.1.call-start
  7.2 0.9 copy-done
  8.1 1.3 multiply_convert_fusion
  9.4 0.0 copy-done.4
  9.4 0.9 fusion.47
  10.2 0.0 copy-start.2
  10.2 0.0 all-reduce.5.cloned.1.call-update
  10.3 0.0 all-gather.3.cloned.1.call-start
  10.3 0.8 copy-done.2
  11.1 0.0 copy-start.5
  11.1 0.1 fusion
  11.3 0.6 copy-done.5
  11.9 0.1 fusion.13
  12.0 0.1 fusion.14
  12.1 0.1 fusion.1
  12.2 32.6 %all_gather.9 = bf16[256,512]{1,0:T(8,128)(2,1)S(1)} all-gather(bf16[32,512]{1,0:T(8,128)(2,1)S(1)} %fusion.14), channel_id=1, replica_groups=mesh['wide'=8,'mp'=4] {'wide'}, dimensions={0}, use_global_device_ids=true | all-gather | bytes 294912 | tf_op jit(solution)/shard_map/all_gather | solution.py:92
  44.8 1.1 all-reduce.5.cloned.1.call-done
  45.9 0.0 copy-start.1
  45.9 1.1 multiply_reduce_fusion.1
  47.1 0.0 copy-done.1
  47.1 0.1 fusion.43
  47.2 0.0 copy-start.6
  47.2 0.3 fusion.2
  47.5 0.4 copy-done.6
  47.8 0.1 multiply_reduce_fusion.2
  48.0 5.8 %all-reduce.1 = (f32[128]{0:T(128)S(1)}, f32[128]{0:T(128)S(1)}, f32[128]{0:T(128)S(1)}, f32[128]{0:T(128)S(1)}) all-reduce(f32[128]{0:T(128)S(1)} %get-tuple-element.46, f32[128]{0:T(128)S(1)} %get-tuple-element.47, f32[128]{0:T(128)S(1)} %get-tuple-element.48, f32[128]{0:T(128)S(1)} %get-tuple-element.45), channel_id=1, replica_groups=mesh['wide'=8,'mp'=4] {'mp'}, use_global_device_ids=true, to_apply=%region_11.12 | all-reduce | flops 512 | bytes 4096 | tf_op jit(solution)/shard_map/psum | solution.py:94
  53.7 1.0 fusion.11
  54.7 0.0 all-gather.3.cloned.1.call-update
  54.7 0.0 all-reduce.7.cloned.1.call-start
  54.8 16.8 %all-gather.3.cloned.1.call-done = f32[512,512]{1,0:T(8,128)} async-done(((f32[128,512]{1,0:T(8,128)}), f32[512,512]{1,0:T(8,128)}) %all-gather.3.cloned.1.call-update) | async-done | bytes 1048592 | tf_op jit(solution)/shard_map/all_gather | solution.py:98
  71.6 1.3 reduce_sum.102
  73.0 0.2 multiply_reduce_fusion
  73.2 0.1 divide_convert_fusion
  73.3 0.9 fusion.48
  74.2 1.3 convolution_bitcast_fusion
  75.5 0.0 all-reduce.7.cloned.1.call-update
  75.5 0.6 subtract_reduce_fusion
  76.1 22.2 %psum.61 = f32[]{:T(128)} all-reduce(f32[]{:T(128)} %subtract_reduce_fusion), channel_id=1, replica_groups=mesh['wide'=8,'mp'=4] {'wide'}, use_global_device_ids=true, to_apply=%region_13.14 | all-reduce | flops 1 | bytes 8 | tf_op jit(solution)/shard_map/psum | solution.py:108
  99.0 50.5 %all-reduce.7.cloned.1.call-done = (f32[768,128]{0,1:T(8,128)}, f32[128,512]{1,0:T(8,128)}) async-done(((f32[768,128]{0,1:T(8,128)}, f32[128,512]{1,0:T(8,128)}), (f32[768,128]{0,1:T(8,128)}, f32[128,512]{1,0:T(8,128)})) %all-reduce.7.cloned.1.call-update) | async-done | bytes 655376 | tf_op jit(solution)/shard_map/psum | solution.py:108
  149.5 0.0 copy-start.3
  149.5 2.0 %copy.9 = f32[768,128]{1,0:T(8,128)} copy(f32[768,128]{0,1:T(8,128)} %get-tuple-element.58) | data formatting | bytes 786432
  151.5 0.0 copy-done.3
  151.5 0.7 copy.13
  (4 shorter events, 0.0 us)
Async XLA Ops:
  7.2 0.9 copy-start
  7.2 2.2 %copy-start.4 = (bf16[128,512]{1,0:T(8,128)(2,1)S(1)}, bf16[128,512]{1,0:T(8,128)(2,1)}, u32[]{:S(2)}) copy-start(bf16[128,512]{1,0:T(8,128)(2,1)} %param.10) | copy-start | bytes 393220
  7.2 38.7 %all-reduce.5.cloned.1.call-start = ((), (), s32[]{:S(2)}) async-start(), calls=%async_computation | async-start | bytes 524288 | tf_op jit(solution)/shard_map/psum | solution.py:43
  10.2 0.9 copy-start.2
  10.3 61.4 %all-gather.3.cloned.1.call-start = ((), (), s32[]{:S(2)}) async-start(), calls=%async_computation.1 | async-start | bytes 1310720 | tf_op jit(solution)/shard_map/all_gather | solution.py:98
  11.1 0.8 copy-start.5
  45.9 1.1 copy-start.1
  47.2 0.7 copy-start.6
  54.7 94.8 %all-reduce.7.cloned.1.call-start = ((), (), s32[]{:S(2)}) async-start(), calls=%async_computation.2 | async-start | bytes 1310720 | tf_op jit(solution)/shard_map/psum | solution.py:108
  149.5 2.0 %copy-start.3 = (f32[128,512]{1,0:T(8,128)S(1)}, f32[128,512]{1,0:T(8,128)}, u32[]{:S(2)}) copy-start(f32[128,512]{1,0:T(8,128)} %get-tuple-element.77) | copy-start | bytes 786436
Sparse Core Ops, SparseCore 0:
  10.9 34.9 all-reduce.4
  54.9 16.7 all-gather.2
  75.7 73.7 all-reduce.6
